TPU v7x, 512 devices: a whole 4x4x16 slice. The times are simulated.
512 devices in a mesh: row: 64 (over y, z), col: 8 (over x, core).
Axes of the slice: x: 4, y: 4, z: 16, core: 2. Of those that a mesh axis runs over, the one named last changes fastest.
Arguments:
- sketch: bfloat16 [65536, 128], P(('row', 'col')), may hold values from -6 to 6
- degree: float32 [65536], P(('row', 'col')), may hold values from 1 to 64
- block_vals: bfloat16 [64, 8, 16, 128, 128], P('row', 'col'), may hold values from -0.125 to 0.125
- block_rows: int32 [64, 8, 16], P('row', 'col'), may hold values from 0 to 7
- block_cols: int32 [64, 8, 16], P('row', 'col'), may hold values from 0 to 63
- live_count: int32 [64, 8], P('row', 'col'), may hold values from 2 to 16, as said below
Outputs:
- basis: float32 [65536, 128], P(('row', 'col'))
- factor: float32 [128, 128], replicated
Inputs may be any that keep to these rules, and one draw needn't show every extreme that they name: Slots at or past live_count of a device are ignored; some device has all 16 slots live.
All inputs are finite; a program needn't handle non-finite values.
Results may differ from a plain program's by a relative error of at most 0.003.
Values may be sent and summed in bfloat16 or wider, within the bound.
A program may use at most 64 MiB of HBM per device.

v0:
```python
import jax
import jax.numpy as jnp
from jax import lax
from jax.sharding import PartitionSpec as P


def local(sketch, degree, block_vals, block_rows, block_cols, live_count):
    rows_dev = sketch.shape[0]
    rank = sketch.shape[1]
    slots = block_vals.shape[2]
    blk = block_vals.shape[3]
    n_row = lax.axis_size("row")
    n_col = lax.axis_size("col")
    row_blocks = rows_dev * n_col // blk
    col_blocks = rows_dev * n_row // blk
    nodes = rows_dev * n_row * n_col
    values = block_vals.reshape(slots, blk, blk)
    rows_here = block_rows.reshape(slots)
    cols_here = block_cols.reshape(slots)
    live_total = live_count.reshape(())
    slot_ids = lax.iota(jnp.int32, slots)
    block_ids = lax.iota(jnp.int32, row_blocks)
    live = slot_ids < live_total
    table = ((rows_here[:, None] == block_ids[None, :]) & live[:, None]).astype(jnp.float32)
    scale = lax.rsqrt(degree)
    basis = sketch.astype(jnp.float32)
    moved = (scale[:, None] * basis).astype(jnp.bfloat16)
    stripe = lax.all_gather(moved, "row", axis=0, tiled=True)
    stripe_blocks = stripe.reshape(col_blocks, blk, rank)
    picked = jnp.take(stripe_blocks, cols_here, axis=0)
    products = jnp.einsum("nab,nbk->nak", values, picked, preferred_element_type=jnp.float32)
    partial_value = jnp.einsum("nr,nak->rak", table, products, precision=lax.Precision.HIGHEST)
    partial_value = partial_value.reshape(row_blocks * blk, rank)
    summed = lax.psum_scatter(partial_value, "col", scatter_dimension=0, tiled=True)
    image = scale[:, None] * summed
    local_gram = jnp.dot(image.T, image, precision=lax.Precision.HIGHEST)
    gram = lax.psum(local_gram, ("row", "col"))
    gram = gram / nodes
    lower = jnp.linalg.cholesky(gram)
    basis = jax.scipy.linalg.solve_triangular(lower, image.T, lower=True).T
    return (basis, lower.T)


def solution(mesh):
    in_specs = (
        P(("row", "col"), None),
        P(("row", "col")),
        P("row", "col", None, None, None),
        P("row", "col", None),
        P("row", "col", None),
        P("row", "col"),
    )
    out_specs = (P(("row", "col"), None), P())
    return jax.shard_map(local, mesh=mesh, in_specs=in_specs, out_specs=out_specs, check_vma=False)
```

profile of v0, /device:TPU:1, one launch (start us, length us, event | category | flops | bytes accessed | tf_op | source)
XLA Modules:
  0.0 684.9 jit_solution(11248738669199386243)
XLA Ops:
  7.2 0.0 copy-start
  7.2 0.0 all-gather.2.cloned.1.call-start
  7.2 0.7 rsqrt.3
  7.9 1.5 multiply_convert_fusion
  9.4 0.0 all-gather.2.cloned.1.call-update
  9.4 0.0 reduce-scatter.2.cloned.1.call-start
  10.1 0.7 fusion.21
  10.8 0.7 compare_and_fusion
  11.5 136.5 %all-gather.2.cloned.1.call-done = bf16[8192,128]{1,0:T(8,128)(2,1)} async-done(((bf16[128,128]{1,0:T(8,128)(2,1)}), bf16[8192,128]{1,0:T(8,128)(2,1)}) %all-gather.2.cloned.1.call-update) | async-done | bytes 2097168 | tf_op jit(solution)/shard_map/all_gather | solution.py:28
  148.0 2.2 gather_fusion
  150.2 0.0 copy-done
  150.3 0.0 copy-start.1
  150.3 0.7 fusion.2
  151.0 0.5 copy.15
  151.5 0.0 copy-done.1
  151.5 0.5 fusion
  152.0 0.9 copy.11
  152.9 0.0 reduce-scatter.2.cloned.1.call-update
  152.9 0.0 all-reduce.2.cloned.1.call-start
  152.9 43.5 %reduce-scatter.2.cloned.1.call-done = f32[128,128]{1,0:T(8,128)} async-done(((f32[1024,128]{1,0:T(8,128)}), f32[128,128]{1,0:T(8,128)}) %reduce-scatter.2.cloned.1.call-update) | async-done | bytes 65552 | tf_op jit(solution)/shard_map/reduce_scatter | solution.py:34
  196.4 1.9 fusion.11
  198.3 0.0 all-reduce.2.cloned.1.call-update
  198.4 452.9 %all-reduce.2.cloned.1.call-done = f32[128,128]{0,1:T(8,128)} async-done(((f32[128,128]{0,1:T(8,128)}), f32[128,128]{0,1:T(8,128)}) %all-reduce.2.cloned.1.call-update) | async-done | bytes 65552 | tf_op jit(solution)/shard_map/psum | solution.py:37
  651.2 0.8 broadcast_multiply_fusion
  652.1 0.1 copy.13
  652.1 0.9 fusion.9
  653.0 11.7 %cholesky.16 = f32[128,128]{1,0:T(8,128)S(1)} custom-call(f32[128,128]{1,0:T(8,128)S(1)} %fusion.9), custom_call_target="Cholesky" | custom-call | tf_op jit(solution)/shard_map/jit(cholesky)/cholesky | solution.py:39
  664.8 0.6 compare_reduce_fusion
  665.4 0.7 fusion.13
  666.1 9.8 %custom-call.7 = f32[1,128,128]{1,2,0:T(8,128)S(1)} custom-call(f32[1,128,128]{2,1,0:T(8,128)S(1)} %get-tuple-element.7), custom_call_target="InvertDiagBlocksLowerTriangular" | custom-call | tf_op jit(solution)/shard_map/jit(_solve_triangular)/triangular_solve | solution.py:40
  675.9 0.7 copy.14
  676.6 1.7 fusion.7
  (3 shorter events, 0.1 us)
Async XLA Ops:
  7.2 143.1 %copy-start = (bf16[1,1,16,128,128]{4,3,2,1,0:T(8,128)(2,1)S(1)}, bf16[1,1,16,128,128]{4,3,2,1,0:T(8,128)(2,1)}, u32[]{:S(2)}) copy-start(bf16[1,1,16,128,128]{4,3,2,1,0:T(8,128)(2,1)} %param.8) | copy-start | bytes 1572868
  7.2 140.8 %all-gather.2.cloned.1.call-start = ((), (), s32[]{:S(2)}) async-start(), calls=%async_computation.1 | async-start | bytes 2129920 | tf_op jit(solution)/shard_map/all_gather | solution.py:28
  9.4 187.0 %reduce-scatter.2.cloned.1.call-start = ((), (), s32[]{:S(2)}) async-start(), calls=%async_computation.2 | async-start | bytes 589824 | tf_op jit(solution)/shard_map/reduce_scatter | solution.py:34
  150.3 1.2 copy-start.1
  152.9 498.3 %all-reduce.2.cloned.1.call-start = ((), (), s32[]{:S(2)}) async-start(), calls=%async_computation.3 | async-start | bytes 131072 | tf_op jit(solution)/shard_map/psum | solution.py:37
Sparse Core Ops, SparseCore 0:
  11.5 136.4 all-gather.1
  153.0 43.3 reduce-scatter.1
  202.5 448.7 all-reduce.1
where the time goes:
time: 685 us
  waiting for transfers between devices  633 us (92%)
  other arithmetic  27.3 us (4%)
  between operations  14.5 us (2%)
    psum x1, waiting for transfers between devices, local(): gram = lax.psum(local_gram, ('row', 'col'))  453 us
    all_gather x1, waiting for transfers between devices, local(): stripe = lax.all_gather(moved, 'row', axis=0, tiled=True)  137 us
    reduce_scatter x1, waiting for transfers between devices, local(): lax.psum_scatter(partial_value, 'col', scatter_dimension=0, tiled=True)  43.5 us
  transfers between devices with their start and end apart: 3, of which 3 were waited for; matrix products, arithmetic and copies ran while one was open for 0% of the time, Pallas kernels for 0%

commit v1 on v0

v1 whole, which is shorter than its diff:
```python
import functools

import jax
import jax.numpy as jnp
from jax import lax
from jax.experimental import pallas as pl
from jax.experimental.pallas import tpu as pltpu
from jax.sharding import PartitionSpec as P

MESH = pl.DeviceIdType.MESH
HIGHEST = lax.Precision.HIGHEST
NX, NY, NZ = 4, 4, 16
BLK = 128
SLOTS = 16
ZFIRST = 128


def halves(lo, hi):
    mid = lo + (hi - lo + 31) // 32 * 16
    return {1: (lo, mid), -1: (mid, hi)}


def gather_plan():
    plan = []
    if ZFIRST > 0:
        half = halves(0, ZFIRST)
        for s in range(NZ // 2):
            for d in (1, -1):
                lo, hi = (0, ZFIRST) if s < NZ // 2 - 1 else half[d]
                plan.append((s, 0, d, 0, -d * s, lo, hi))
        for oz in range(1 - NZ // 2, NZ // 2 + 1):
            for d in (1, -1):
                plan.append((abs(oz) + 0.2, d, 0, 0, oz, 0, ZFIRST))
                lo, hi = half[d]
                plan.append((abs(oz) + 1.1, d, 0, -d, oz, lo, hi))
    if ZFIRST < BLK:
        half = halves(ZFIRST, BLK)
        for d in (1, -1):
            plan.append((0, d, 0, 0, 0, ZFIRST, BLK))
            lo, hi = half[d]
            plan.append((1, d, 0, -d, 0, lo, hi))
        for oy, start in ((0, 0), (-1, 1), (1, 1), (2, 2)):
            for s in range(NZ // 2):
                for d in (1, -1):
                    lo, hi = (ZFIRST, BLK) if s < NZ // 2 - 1 else half[d]
                    plan.append((start + s + 0.3, 0, d, oy, -d * s, lo, hi))
    return sorted(plan, key=lambda m: m[0])


def wrap(value, n):
    value = value % n
    return value - n if value > n // 2 else value


PLAN = gather_plan()
N_PLAN = len(PLAN)


def row_of(y, z):
    return lax.rem(y + 4 * NY, NY) * NZ + lax.rem(z + 4 * NZ, NZ)


def comm_kernel(sk_ref, deg_ref, vals_hbm, rows_ref, cols_ref, live_ref, gram_ref, image_ref,
                gat, vals, prods, part, crecv, comb, xrecv, glocal, rsbuf, zbuf, tile,
                vsem, gs, gr, cs, cr, xs, xr, rs_s, rs_r, z_s, z_r, ag_s, ag_r):
    row = lax.axis_index("row")
    col = lax.axis_index("col")
    y, z = row // NZ, lax.rem(row, NZ)
    x, core = col // 2, lax.rem(col, 2)

    barrier = pltpu.get_barrier_semaphore()
    peers = [(row_of(y, z + 1), col), (row_of(y, z - 1), col), (row_of(y + 1, z), col), (row_of(y - 1, z), col)]
    peers += [(row, lax.rem(col + k, 2 * NX)) for k in range(1, 2 * NX)]
    for peer in peers:
        pl.semaphore_signal(barrier, inc=1, device_id=peer, device_id_type=MESH)
    load_vals = pltpu.make_async_copy(vals_hbm, vals, vsem)
    load_vals.start()

    ids_r = lax.broadcasted_iota(jnp.int32, (BLK, BLK), 0)
    ids_c = lax.broadcasted_iota(jnp.int32, (BLK, BLK), 1)
    spread = jnp.where(ids_r == ids_c, jnp.broadcast_to(deg_ref[...], (BLK, BLK)), 0.0)
    scale = lax.rsqrt(jnp.sum(spread, axis=1, keepdims=True))
    gat[row] = (scale * sk_ref[...].astype(jnp.float32)).astype(jnp.bfloat16)
    pl.semaphore_wait(barrier, len(peers))

    def message(i):
        _, dy, dz, oy, oz, lo, hi = PLAN[i]
        block = gat.at[row_of(y + oy, z + oz), pl.ds(lo, hi - lo), :]
        return pltpu.make_async_remote_copy(
            src_ref=block, dst_ref=block, send_sem=gs.at[i], recv_sem=gr.at[i],
            device_id=(row_of(y + dy, z + dz), col), device_id_type=MESH)

    def landed(i):
        _, dy, dz, oy, oz, lo, hi = PLAN[i]
        block = gat.at[row_of(y + oy - dy, z + oz - dz), pl.ds(lo, hi - lo), :]
        pltpu.make_async_remote_copy(
            src_ref=block, dst_ref=block, send_sem=gs.at[i], recv_sem=gr.at[i],
            device_id=(row_of(y + dy, z + dz), col), device_id_type=MESH).wait_recv()

    waited = set()
    for i, (_, dy, dz, oy, oz, lo, hi) in enumerate(PLAN):
        for j, (_, ey, ez, py, pz, plo, phi) in enumerate(PLAN):
            here = (wrap(py - ey, NY), wrap(pz - ez, NZ)) == (wrap(oy, NY), wrap(oz, NZ))
            if here and plo < hi and lo < phi and j not in waited:
                landed(j)
                waited.add(j)
        message(i).start()
    for j in range(N_PLAN):
        if j not in waited:
            landed(j)

    load_vals.wait()
    for s in range(SLOTS):
        picked = gat[cols_ref[s]]
        prods[s] = jnp.dot(vals[s], picked, preferred_element_type=jnp.float32)
    live = live_ref[0]
    for r in range(2 * NX):
        weights = [jnp.where((rows_ref[s] == r) & (s < live), 1.0, 0.0) for s in range(SLOTS)]
        for k in range(BLK // 16):
            lines = pl.ds(k * 16, 16)
            total = weights[0] * prods[0, lines, :]
            for s in range(1, SLOTS):
                total = total + weights[s] * prods[s, lines, :]
            part[r % 2, r // 2, lines, :] = total

    other = 1 - core
    swap = pltpu.make_async_remote_copy(
        src_ref=part.at[other], dst_ref=crecv, send_sem=cs, recv_sem=cr,
        device_id=(row, x * 2 + other), device_id_type=MESH)
    swap.start()
    swap.wait_recv()
    sends = []
    for k in (2, 1, 3):
        to = lax.rem(x + k, NX)
        comb[k] = part[core, to] + crecv[to]
        send = pltpu.make_async_remote_copy(
            src_ref=comb.at[k], dst_ref=xrecv.at[k], send_sem=xs.at[k], recv_sem=xr.at[k],
            device_id=(row, to * 2 + core), device_id_type=MESH)
        send.start()
        sends.append(send)
    total = part[core, x] + crecv[x]
    for send in (sends[1], sends[2], sends[0]):
        send.wait_recv()
    for k in (1, 2, 3):
        total = total + xrecv[k]
    image = scale * total
    image_ref[...] = image
    glocal[...] = lax.dot_general(image, image, (((0,), (0,)), ((), ())), precision=HIGHEST,
                                  preferred_element_type=jnp.float32)

    chip = x * NY + y
    me = chip * 2 + core
    keeper = lax.rem(x + y, 2)
    owner = core == keeper

    def plane(t):
        tx, ty = t // NY, lax.rem(t, NY)
        return tx, ty, lax.rem(tx + ty, 2)

    def scatter(k):
        t = lax.rem(chip + k, NX * NY)
        tx, ty, tc = plane(t)
        return pltpu.make_async_remote_copy(
            src_ref=glocal.at[pl.ds(pl.multiple_of(t * 8, 8), 8), :], dst_ref=rsbuf.at[me],
            send_sem=rs_s.at[k], recv_sem=rs_r.at[me],
            device_id=(row_of(ty, z), tx * 2 + tc), device_id_type=MESH)

    def keep(k):
        t = lax.rem(chip + k, NX * NY)
        tx, ty, _ = plane(t)
        return tx, ty, t

    for k in list(range(1, NX * NY)):
        scatter(k).start()

    @pl.when(jnp.logical_not(owner))
    def _():
        scatter(0).start()

    mine = pl.ds(pl.multiple_of(chip * 8, 8), 8)

    @pl.when(owner)
    def _():
        total = glocal[mine, :]
        for k in range(1, 2 * NX * NY):
            src = lax.rem(me + k, 2 * NX * NY)
            pltpu.make_async_remote_copy(
                src_ref=rsbuf.at[src], dst_ref=rsbuf.at[src], send_sem=rs_s.at[0], recv_sem=rs_r.at[src],
                device_id=(row, x * 2 + other), device_id_type=MESH).wait_recv()
        for k in range(1, 2 * NX * NY):
            total = total + rsbuf[lax.rem(me + k, 2 * NX * NY)]
        zbuf[z] = total

        def along(k):
            return pltpu.make_async_remote_copy(
                src_ref=zbuf.at[z], dst_ref=zbuf.at[z], send_sem=z_s.at[k], recv_sem=z_r.at[z],
                device_id=(row_of(y, z + k), col), device_id_type=MESH)

        order = sorted(range(1, NZ), key=lambda k: -min(k, NZ - k))
        for k in order:
            along(k).start()
        for k in reversed(order):
            src = lax.rem(z + k, NZ)
            pltpu.make_async_remote_copy(
                src_ref=zbuf.at[src], dst_ref=zbuf.at[src], send_sem=z_s.at[k], recv_sem=z_r.at[src],
                device_id=(row_of(y, z + k), col), device_id_type=MESH).wait_recv()
        total = zbuf[0]
        for k in range(1, NZ):
            total = total + zbuf[k]
        gram_ref[mine, :] = total

        def back(k):
            if k == 0:
                device = (row, x * 2 + other)
            else:
                t = lax.rem(chip + k // 2, NX * NY)
                device = (row_of(lax.rem(t, NY), z), t // NY * 2 + k % 2)
            return pltpu.make_async_remote_copy(
                src_ref=gram_ref.at[mine, :], dst_ref=gram_ref.at[mine, :], send_sem=ag_s.at[k],
                recv_sem=ag_r.at[chip], device_id=device, device_id_type=MESH)

        spots = [0] + list(range(2, 2 * NX * NY))
        for k in spots[::-1]:
            back(k).start()
        for k in order:
            along(k).wait_send()
        for k in spots:
            back(k).wait_send()

    def arrive(t):
        lines = pl.ds(pl.multiple_of(t * 8, 8), 8)
        pltpu.make_async_remote_copy(
            src_ref=gram_ref.at[lines, :], dst_ref=gram_ref.at[lines, :], send_sem=ag_s.at[0],
            recv_sem=ag_r.at[t], device_id=(row, x * 2 + other), device_id_type=MESH).wait_recv()

    for k in range(1, NX * NY):
        arrive(lax.rem(chip + k, NX * NY))

    @pl.when(jnp.logical_not(owner))
    def _():
        arrive(chip)
        scatter(0).wait_send()

    for i in range(N_PLAN):
        message(i).wait_send()
    swap.wait_send()
    for send in sends:
        send.wait_send()
    for k in range(1, NX * NY):
        scatter(k).wait_send()


def factor_kernel(nodes, gram_ref, image_ref, basis_ref, factor_ref, inv_ref):
    tiles = BLK // 8
    left = [gram_ref[pl.ds(k * 8, 8), :] * (1.0 / nodes) for k in range(tiles)]
    row_ids = lax.broadcasted_iota(jnp.int32, (8, BLK), 0)
    lane_ids = lax.broadcasted_iota(jnp.int32, (8, BLK), 1)
    right = [jnp.where(row_ids + 8 * k == lane_ids, 1.0, 0.0) for k in range(tiles)]
    for j in range(BLK):
        k0, r = divmod(j, 8)
        pivot = left[k0][r:r + 1, j:j + 1]
        inv = lax.rsqrt(pivot)
        up_left = left[k0][r:r + 1, :] * inv
        up_right = right[k0][r:r + 1, :] * inv
        factor_ref[pl.ds(j, 1), :] = jnp.where(lane_ids[:1] >= j, up_left, 0.0)
        inv_ref[pl.ds(j, 1), :] = up_right
        for k in range(k0, tiles):
            by = left[k][:, j:j + 1] * inv
            if k == k0:
                if r == 7:
                    continue
                by = jnp.where(row_ids[:, :1] > r, by, 0.0)
            left[k] = left[k] - by * up_left
            right[k] = right[k] - by * up_right
    basis_ref[...] = lax.dot_general(image_ref[...], inv_ref[...], (((1,), (1,)), ((), ())), precision=HIGHEST,
                                     preferred_element_type=jnp.float32)


def local(sketch, degree, block_vals, block_rows, block_cols, live_count):
    f32 = jnp.float32
    square = jax.ShapeDtypeStruct((BLK, BLK), f32)
    vmem = pl.BlockSpec(memory_space=pltpu.VMEM)
    smem = pl.BlockSpec(memory_space=pltpu.SMEM)
    dma = pltpu.SemaphoreType.DMA
    gram, image = pl.pallas_call(
        comm_kernel,
        out_shape=(square, square),
        in_specs=[vmem, vmem, pl.BlockSpec(memory_space=pl.ANY), smem, smem, smem],
        out_specs=(vmem, vmem),
        scratch_shapes=[
            pltpu.VMEM((NY * NZ, BLK, BLK), jnp.bfloat16),
            pltpu.VMEM((SLOTS, BLK, BLK), jnp.bfloat16),
            pltpu.VMEM((SLOTS, BLK, BLK), f32),
            pltpu.VMEM((2, NX, BLK, BLK), f32),
            pltpu.VMEM((NX, BLK, BLK), f32),
            pltpu.VMEM((NX, BLK, BLK), f32),
            pltpu.VMEM((NX, BLK, BLK), f32),
            pltpu.VMEM((BLK, BLK), f32),
            pltpu.VMEM((2 * NX * NY, 8, BLK), f32),
            pltpu.VMEM((NZ, 8, BLK), f32),
            pltpu.VMEM((8, BLK), f32),
            dma, dma((N_PLAN,)), dma((N_PLAN,)), dma, dma, dma((NX,)), dma((NX,)),
            dma((NX * NY,)), dma((2 * NX * NY,)), dma((NZ,)), dma((NZ,)), dma((2 * NX * NY,)), dma((NX * NY,)),
        ],
        compiler_params=pltpu.CompilerParams(collective_id=0, has_side_effects=True),
        name="spread",
    )(sketch, degree.reshape(1, BLK), block_vals.reshape(SLOTS, BLK, BLK), block_rows.reshape(SLOTS),
      block_cols.reshape(SLOTS), live_count.reshape(1))
    nodes = BLK * lax.axis_size("row") * lax.axis_size("col")
    return pl.pallas_call(
        functools.partial(factor_kernel, nodes),
        out_shape=(square, square),
        in_specs=[vmem, vmem],
        out_specs=(vmem, vmem),
        scratch_shapes=[pltpu.VMEM((BLK, BLK), f32)],
        name="orthonormalize",
    )(gram, image)


def solution(mesh):
    in_specs = (
        P(("row", "col"), None),
        P(("row", "col")),
        P("row", "col", None, None, None),
        P("row", "col", None),
        P("row", "col", None),
        P("row", "col"),
    )
    out_specs = (P(("row", "col"), None), P())
    return jax.shard_map(local, mesh=mesh, in_specs=in_specs, out_specs=out_specs, check_vma=False)
```

time: 685 us -> 95 us (0.14)
  waiting for transfers between devices: 633 us -> 0 us
  Pallas kernels: 0 us -> 93.5 us
  other arithmetic: 27.3 us -> 0 us
  between operations: 14.5 us -> 1.29 us
    psum x1 -> x0, waiting for transfers between devices: 453 us -> none  [local(): gram = lax.psum(local_gram, ('row', 'col'))]
    all_gather x1 -> x0, waiting for transfers between devices: 137 us -> none  [local(): stripe = lax.all_gather(moved, 'row', axis=0, tiled=True)]
    pallas_call x0 -> x2, Pallas kernels: none -> 93.5 us  [the longest x1 81 us: local(): pl.pallas_call(comm_kernel, out_shape=(square, square), in_specs=[vmem, v...]
    reduce_scatter x1 -> x0, waiting for transfers between devices: 43.5 us -> none  [local(): lax.psum_scatter(partial_value, 'col', scatter_dimension=0, tiled=True)]
    another operation x4 -> x0, other arithmetic: 22.2 us -> none  [the longest x3 12.4 us: local(): lower = jnp.linalg.cholesky(gram)]
  transfers between devices with their start and end apart: 3 -> 0, of which waited for: 3 -> 0; matrix products, arithmetic and copies ran while one was open for 0% -> 0% of each run, Pallas kernels for 0% -> 0%
where the time goes in v1:
time: 95 us; the launch traced here: 94.8 us
  Pallas kernels  93.5 us (98%)
  between operations  1.29 us (1%)
    pallas_call x1, Pallas kernels, local(): pl.pallas_call(comm_kernel, out_shape=(square, square), in_specs=[vmem, v...  81 us
    pallas_call x1, Pallas kernels, local(): pl.pallas_call(functools.partial(factor_kernel, nodes), out_shape=(square...  12.4 us

profile of v1, /device:TPU:1, one launch (start us, length us, event | category | flops | bytes accessed | tf_op | source)
XLA Modules:
  0.0 94.8 jit_solution(13073310835008918987)
XLA Ops:
  1.3 81.0 %spread.1 = (f32[128,128]{1,0:T(8,128)}, f32[128,128]{1,0:T(8,128)}) custom-call(bf16[128,128]{1,0:T(8,128)(2,1)} %sk_ref.1, f32[1,128]{1,0:T(1,128)} %bitcast.7, bf16[16,128,128]{2,1,0:T(8,128)(2,1)} %bitcast.6, s32[16]{0:T(128)} %bitcast.8, s32[16]{0:T(128)} %bitcast.9, s32[1]{0:T(128)} %bitcast.5.live_ref), custom_call_target="tpu_custom_call" | custom-call | tf_op jit(solution)/shard_map/spread/pallas_call | solution.py:285
  82.3 12.4 %orthonormalize.1 = (f32[128,128]{1,0:T(8,128)}, f32[128,128]{1,0:T(8,128)}) custom-call(f32[128,128]{1,0:T(8,128)} %get-tuple-element.4.gram_ref, f32[128,128]{1,0:T(8,128)} %get-tuple-element.5.image_ref), custom_call_target="tpu_custom_call" | custom-call | tf_op jit(solution)/shard_map/orthonormalize/pallas_call | solution.py:310

commit v2 on v1

--- a/solution.py
+++ b/solution.py
@@ -12,39 +12,87 @@
 NX, NY, NZ = 4, 4, 16
 BLK = 128
 SLOTS = 16
-ZFIRST = 128
-
-
-def halves(lo, hi):
-    mid = lo + (hi - lo + 31) // 32 * 16
-    return {1: (lo, mid), -1: (mid, hi)}
-
-
-def gather_plan():
-    plan = []
-    if ZFIRST > 0:
-        half = halves(0, ZFIRST)
-        for s in range(NZ // 2):
-            for d in (1, -1):
-                lo, hi = (0, ZFIRST) if s < NZ // 2 - 1 else half[d]
-                plan.append((s, 0, d, 0, -d * s, lo, hi))
-        for oz in range(1 - NZ // 2, NZ // 2 + 1):
-            for d in (1, -1):
-                plan.append((abs(oz) + 0.2, d, 0, 0, oz, 0, ZFIRST))
-                lo, hi = half[d]
-                plan.append((abs(oz) + 1.1, d, 0, -d, oz, lo, hi))
-    if ZFIRST < BLK:
-        half = halves(ZFIRST, BLK)
-        for d in (1, -1):
-            plan.append((0, d, 0, 0, 0, ZFIRST, BLK))
-            lo, hi = half[d]
-            plan.append((1, d, 0, -d, 0, lo, hi))
-        for oy, start in ((0, 0), (-1, 1), (1, 1), (2, 2)):
-            for s in range(NZ // 2):
-                for d in (1, -1):
-                    lo, hi = (ZFIRST, BLK) if s < NZ // 2 - 1 else half[d]
-                    plan.append((start + s + 0.3, 0, d, oy, -d * s, lo, hi))
-    return sorted(plan, key=lambda m: m[0])
+
+PLAN = (
+    (1, 0, 0, 0, 1, 96, 128),
+    (-1, 0, 0, 0, 1, 96, 128),
+    (0, 3, 0, 0, 1, 0, 96),
+    (0, -3, 0, 0, 1, 0, 96),
+    (0, 1, 0, 0, 1, 0, 96),
+    (0, -1, 0, 0, 1, 0, 96),
+    (1, 0, 0, 0, 1, 0, 96),
+    (-1, 0, 0, 0, 1, 0, 96),
+    (1, 0, -1, 0, 1, 96, 112),
+    (-1, 0, 1, 0, 1, 112, 128),
+    (1, 0, -1, 0, 1, 0, 48),
+    (-1, 0, 1, 0, 1, 48, 96),
+    (0, 3, 0, -3, 1, 0, 96),
+    (0, -3, 0, 3, 1, 0, 96),
+    (0, -1, 0, -3, 1, 0, 96),
+    (0, 1, 0, -3, 1, 0, 96),
+    (0, 3, None, 0, 1, 96, 128),
+    (0, -3, None, 0, 1, 96, 128),
+    (0, 1, 0, 3, 1, 0, 96),
+    (0, -1, 0, 3, 1, 0, 96),
+    (1, 0, 0, 1, 1, 0, 96),
+    (-1, 0, 0, 1, 1, 0, 96),
+    (1, 0, 0, -1, 1, 0, 96),
+    (-1, 0, 0, -1, 1, 0, 96),
+    (0, 1, None, 0, 1, 96, 128),
+    (0, -1, None, 0, 1, 96, 128),
+    (0, 1, 0, -6, 1, 0, 96),
+    (0, -1, 0, 6, 1, 0, 96),
+    (0, -1, 0, -6, 1, 0, 96),
+    (0, 1, 0, 6, 1, 0, 96),
+    (1, 0, 0, -3, 2, 0, 96),
+    (-1, 0, 0, -3, 2, 0, 96),
+    (1, 0, -1, 1, 1, 0, 48),
+    (-1, 0, 1, 1, 1, 48, 96),
+    (1, 0, -1, -1, 1, 0, 48),
+    (-1, 0, 1, -1, 1, 48, 96),
+    (0, 3, None, -3, 1, 96, 128),
+    (0, -3, None, 3, 1, 96, 128),
+    (0, -1, None, -3, 1, 96, 128),
+    (0, 1, None, -3, 1, 96, 128),
+    (0, 1, None, 3, 1, 96, 128),
+    (1, 0, 0, 2, 2, 0, 96),
+    (-1, 0, 0, 2, 2, 0, 96),
+    (0, -1, None, 3, 1, 96, 128),
+    (1, 0, -1, -3, 2, 0, 48),
+    (-1, 0, 1, -3, 2, 48, 96),
+    (0, 1, 0, -7, 1, 0, 48),
+    (0, -1, 0, 7, 1, 48, 96),
+    (1, 0, 0, 6, 2, 0, 96),
+    (-1, 0, 0, 6, 2, 0, 96),
+    (1, 0, 0, 4, 2, 0, 96),
+    (-1, 0, 0, 4, 2, 0, 96),
+    (1, 0, 0, -5, 2, 0, 96),
+    (-1, 0, 0, -5, 2, 0, 96),
+    (1, 0, 0, -7, 2, 0, 96),
+    (-1, 0, 0, -7, 2, 0, 96),
+    (1, 0, -1, 2, 2, 0, 48),
+    (-1, 0, 1, 2, 2, 48, 96),
+    (0, 1, None, -6, 1, 96, 128),
+    (0, -1, None, 6, 1, 96, 128),
+    (0, -1, None, -6, 1, 96, 128),
+    (0, 1, None, 6, 1, 96, 128),
+    (1, 0, -1, 6, 2, 0, 48),
+    (-1, 0, 1, 6, 2, 48, 96),
+    (1, 0, 0, 8, 1, 0, 96),
+    (-1, 0, 0, 8, 1, 0, 96),
+    (1, 0, -1, 4, 2, 0, 48),
+    (-1, 0, 1, 4, 2, 48, 96),
+    (0, 1, None, -7, 1, 96, 112),
+    (0, -1, None, 7, 1, 112, 128),
+    (1, 0, -1, -5, 2, 0, 48),
+    (-1, 0, 1, -5, 2, 48, 96),
+    (1, 0, -1, -7, 2, 0, 48),
+    (-1, 0, 1, -7, 2, 48, 96),
+    (1, 0, -1, 8, 1, 0, 48),
+    (-1, 0, 1, 8, 1, 48, 96),
+)
+N_PLAN = len(PLAN)
+LOW = NZ // 2 - 1
 
 
 def wrap(value, n):
@@ -52,56 +100,64 @@
     return value - n if value > n // 2 else value
 
 
-PLAN = gather_plan()
-N_PLAN = len(PLAN)
-
-
 def row_of(y, z):
     return lax.rem(y + 4 * NY, NY) * NZ + lax.rem(z + 4 * NZ, NZ)
 
 
-def comm_kernel(sk_ref, deg_ref, vals_hbm, rows_ref, cols_ref, live_ref, gram_ref, image_ref,
-                gat, vals, prods, part, crecv, comb, xrecv, glocal, rsbuf, zbuf, tile,
+def comm_kernel(sk_any, deg_any, vals_any, rows_any, cols_any, live_any, gram_ref, image_ref,
+                sk_ref, deg_ref, rows_ref, cols_ref, live_ref, gat, vals, prods, part, crecv, comb, xrecv, glocal, rsbuf, zbuf,
                 vsem, gs, gr, cs, cr, xs, xr, rs_s, rs_r, z_s, z_r, ag_s, ag_r):
     row = lax.axis_index("row")
     col = lax.axis_index("col")
     y, z = row // NZ, lax.rem(row, NZ)
     x, core = col // 2, lax.rem(col, 2)
 
+    loads = [pltpu.make_async_copy(src, dst, vsem.at[i]) for i, (src, dst) in enumerate((
+        (deg_any, deg_ref), (sk_any, sk_ref), (vals_any, vals), (rows_any, rows_ref), (cols_any, cols_ref),
+        (live_any, live_ref)))]
+    for load in loads:
+        load.start()
     barrier = pltpu.get_barrier_semaphore()
-    peers = [(row_of(y, z + 1), col), (row_of(y, z - 1), col), (row_of(y + 1, z), col), (row_of(y - 1, z), col)]
+    moves = sorted({(wrap(d * m[0], NY), wrap(d * m[1], NZ)) for m in PLAN for d in (1, -1)})
+    peers = [(row_of(y + dy, z + dz), col) for dy, dz in moves]
     peers += [(row, lax.rem(col + k, 2 * NX)) for k in range(1, 2 * NX)]
     for peer in peers:
         pl.semaphore_signal(barrier, inc=1, device_id=peer, device_id_type=MESH)
-    load_vals = pltpu.make_async_copy(vals_hbm, vals, vsem)
-    load_vals.start()
-
+    loads[0].wait()
+    loads[1].wait()
     ids_r = lax.broadcasted_iota(jnp.int32, (BLK, BLK), 0)
     ids_c = lax.broadcasted_iota(jnp.int32, (BLK, BLK), 1)
     spread = jnp.where(ids_r == ids_c, jnp.broadcast_to(deg_ref[...], (BLK, BLK)), 0.0)
     scale = lax.rsqrt(jnp.sum(spread, axis=1, keepdims=True))
-    gat[row] = (scale * sk_ref[...].astype(jnp.float32)).astype(jnp.bfloat16)
+    gat[y, LOW] = (scale * sk_ref[...].astype(jnp.float32)).astype(jnp.bfloat16)
     pl.semaphore_wait(barrier, len(peers))
 
+    def blocks(oy, oz, count, lo, hi):
+        ys = slice(None) if oy is None else lax.rem(y + oy + NY, NY)
+        return gat.at[ys, pl.ds(oz + LOW, count), pl.ds(lo, hi - lo), :]
+
     def message(i):
-        _, dy, dz, oy, oz, lo, hi = PLAN[i]
-        block = gat.at[row_of(y + oy, z + oz), pl.ds(lo, hi - lo), :]
+        dy, dz, oy, oz, count, lo, hi = PLAN[i]
         return pltpu.make_async_remote_copy(
-            src_ref=block, dst_ref=block, send_sem=gs.at[i], recv_sem=gr.at[i],
+            src_ref=blocks(oy, oz, count, lo, hi), dst_ref=blocks(oy, wrap(oz - dz, NZ), count, lo, hi),
+            send_sem=gs.at[i], recv_sem=gr.at[i],
             device_id=(row_of(y + dy, z + dz), col), device_id_type=MESH)
 
     def landed(i):
-        _, dy, dz, oy, oz, lo, hi = PLAN[i]
-        block = gat.at[row_of(y + oy - dy, z + oz - dz), pl.ds(lo, hi - lo), :]
+        dy, dz, oy, oz, count, lo, hi = PLAN[i]
+        block = blocks(None if oy is None else oy - dy, wrap(oz - dz, NZ), count, lo, hi)
         pltpu.make_async_remote_copy(
             src_ref=block, dst_ref=block, send_sem=gs.at[i], recv_sem=gr.at[i],
             device_id=(row_of(y + dy, z + dz), col), device_id_type=MESH).wait_recv()
 
+    def places(oy, oz, count):
+        return {(wrap(v, NY), wrap(oz + k, NZ)) for v in (range(NY) if oy is None else (oy,)) for k in range(count)}
+
     waited = set()
-    for i, (_, dy, dz, oy, oz, lo, hi) in enumerate(PLAN):
-        for j, (_, ey, ez, py, pz, plo, phi) in enumerate(PLAN):
-            here = (wrap(py - ey, NY), wrap(pz - ez, NZ)) == (wrap(oy, NY), wrap(oz, NZ))
-            if here and plo < hi and lo < phi and j not in waited:
+    for i, (_, _, oy, oz, count, lo, hi) in enumerate(PLAN):
+        for j, (dy, dz, py, pz, many, plo, phi) in enumerate(PLAN):
+            brought = places(None if py is None else py - dy, pz - dz, many)
+            if j not in waited and plo < hi and lo < phi and brought & places(oy, oz, count):
                 landed(j)
                 waited.add(j)
         message(i).start()
@@ -109,13 +165,15 @@
         if j not in waited:
             landed(j)
 
-    load_vals.wait()
+    for load in loads[2:]:
+        load.wait()
     for s in range(SLOTS):
-        picked = gat[cols_ref[s]]
+        at = cols_ref[0, 0, s]
+        picked = gat[at // NZ, lax.rem(lax.rem(at, NZ) - z + LOW + NZ, NZ)]
         prods[s] = jnp.dot(vals[s], picked, preferred_element_type=jnp.float32)
-    live = live_ref[0]
+    live = live_ref[0, 0]
     for r in range(2 * NX):
-        weights = [jnp.where((rows_ref[s] == r) & (s < live), 1.0, 0.0) for s in range(SLOTS)]
+        weights = [jnp.where((rows_ref[0, 0, s] == r) & (s < live), 1.0, 0.0) for s in range(SLOTS)]
         for k in range(BLK // 16):
             lines = pl.ds(k * 16, 16)
             total = weights[0] * prods[0, lines, :]
@@ -165,11 +223,6 @@
             send_sem=rs_s.at[k], recv_sem=rs_r.at[me],
             device_id=(row_of(ty, z), tx * 2 + tc), device_id_type=MESH)
 
-    def keep(k):
-        t = lax.rem(chip + k, NX * NY)
-        tx, ty, _ = plane(t)
-        return tx, ty, t
-
     for k in list(range(1, NX * NY)):
         scatter(k).start()
 
@@ -280,15 +333,19 @@
     f32 = jnp.float32
     square = jax.ShapeDtypeStruct((BLK, BLK), f32)
     vmem = pl.BlockSpec(memory_space=pltpu.VMEM)
-    smem = pl.BlockSpec(memory_space=pltpu.SMEM)
     dma = pltpu.SemaphoreType.DMA
     gram, image = pl.pallas_call(
         comm_kernel,
         out_shape=(square, square),
-        in_specs=[vmem, vmem, pl.BlockSpec(memory_space=pl.ANY), smem, smem, smem],
+        in_specs=[pl.BlockSpec(memory_space=pl.ANY)] * 6,
         out_specs=(vmem, vmem),
         scratch_shapes=[
-            pltpu.VMEM((NY * NZ, BLK, BLK), jnp.bfloat16),
+            pltpu.VMEM((BLK, BLK), jnp.bfloat16),
+            pltpu.VMEM((1, BLK), f32),
+            pltpu.SMEM((1, 1, SLOTS), jnp.int32),
+            pltpu.SMEM((1, 1, SLOTS), jnp.int32),
+            pltpu.SMEM((1, 1), jnp.int32),
+            pltpu.VMEM((NY, NZ, BLK, BLK), jnp.bfloat16),
             pltpu.VMEM((SLOTS, BLK, BLK), jnp.bfloat16),
             pltpu.VMEM((SLOTS, BLK, BLK), f32),
             pltpu.VMEM((2, NX, BLK, BLK), f32),
@@ -298,14 +355,13 @@
             pltpu.VMEM((BLK, BLK), f32),
             pltpu.VMEM((2 * NX * NY, 8, BLK), f32),
             pltpu.VMEM((NZ, 8, BLK), f32),
-            pltpu.VMEM((8, BLK), f32),
-            dma, dma((N_PLAN,)), dma((N_PLAN,)), dma, dma, dma((NX,)), dma((NX,)),
+            dma((6,)), dma((N_PLAN,)), dma((N_PLAN,)), dma, dma, dma((NX,)), dma((NX,)),
             dma((NX * NY,)), dma((2 * NX * NY,)), dma((NZ,)), dma((NZ,)), dma((2 * NX * NY,)), dma((NX * NY,)),
         ],
         compiler_params=pltpu.CompilerParams(collective_id=0, has_side_effects=True),
         name="spread",
-    )(sketch, degree.reshape(1, BLK), block_vals.reshape(SLOTS, BLK, BLK), block_rows.reshape(SLOTS),
-      block_cols.reshape(SLOTS), live_count.reshape(1))
+    )(sketch, degree.reshape(1, BLK), block_vals.reshape(SLOTS, BLK, BLK), block_rows, block_cols,
+      live_count)
     nodes = BLK * lax.axis_size("row") * lax.axis_size("col")
     return pl.pallas_call(
         functools.partial(factor_kernel, nodes),

time: 95 us -> 80.2 us (0.84)
  Pallas kernels: 93.5 us -> 78.7 us
    pallas_call x1, Pallas kernels: 81 us -> 66.3 us  [local(): pl.pallas_call(comm_kernel, out_shape=(square, square), in_specs=[pl.Bloc...]
where the time goes in v2:
time: 80.2 us; the launch traced here: 80 us
  Pallas kernels  78.7 us (98%)
  between operations  1.29 us (2%)
    pallas_call x1, Pallas kernels, local(): pl.pallas_call(comm_kernel, out_shape=(square, square), in_specs=[pl.Bloc...  66.3 us
    pallas_call x1, Pallas kernels, local(): pl.pallas_call(functools.partial(factor_kernel, nodes), out_shape=(square...  12.4 us

profile of v2, /device:TPU:1, one launch (start us, length us, event | category | flops | bytes accessed | tf_op | source)
XLA Modules:
  0.0 80.0 jit_solution(18087254065707192316)
XLA Ops:
  1.3 66.3 %spread.1 = (f32[128,128]{1,0:T(8,128)}, f32[128,128]{1,0:T(8,128)}) custom-call(bf16[128,128]{1,0:T(8,128)(2,1)} %sk_any.1, f32[1,128]{1,0:T(1,128)} %bitcast.3, bf16[16,128,128]{2,1,0:T(8,128)(2,1)} %bitcast.2, s32[1,1,16]{2,1,0:T(1,128)} %rows_any.1, s32[1,1,16]{2,1,0:T(1,128)} %cols_any.1, s32[1,1]{1,0:T(1,128)S(6)} %copy.8.live_any), custom_call_target="tpu_custom_call" | custom-call | tf_op jit(solution)/shard_map/spread/pallas_call | solution.py:337
  67.6 12.4 %orthonormalize.1 = (f32[128,128]{1,0:T(8,128)}, f32[128,128]{1,0:T(8,128)}) custom-call(f32[128,128]{1,0:T(8,128)} %get-tuple-element.4.gram_ref, f32[128,128]{1,0:T(8,128)} %get-tuple-element.5.image_ref), custom_call_target="tpu_custom_call" | custom-call | tf_op jit(solution)/shard_map/orthonormalize/pallas_call | solution.py:366

commit v3 on v2

--- a/solution.py
+++ b/solution.py
@@ -305,26 +305,45 @@
 
 def factor_kernel(nodes, gram_ref, image_ref, basis_ref, factor_ref, inv_ref):
     tiles = BLK // 8
+    full = (8, BLK)
     left = [gram_ref[pl.ds(k * 8, 8), :] * (1.0 / nodes) for k in range(tiles)]
-    row_ids = lax.broadcasted_iota(jnp.int32, (8, BLK), 0)
-    lane_ids = lax.broadcasted_iota(jnp.int32, (8, BLK), 1)
+    row_ids = lax.broadcasted_iota(jnp.int32, full, 0)
+    lane_ids = lax.broadcasted_iota(jnp.int32, full, 1)
     right = [jnp.where(row_ids + 8 * k == lane_ids, 1.0, 0.0) for k in range(tiles)]
-    for j in range(BLK):
-        k0, r = divmod(j, 8)
-        pivot = left[k0][r:r + 1, j:j + 1]
-        inv = lax.rsqrt(pivot)
-        up_left = left[k0][r:r + 1, :] * inv
-        up_right = right[k0][r:r + 1, :] * inv
-        factor_ref[pl.ds(j, 1), :] = jnp.where(lane_ids[:1] >= j, up_left, 0.0)
-        inv_ref[pl.ds(j, 1), :] = up_right
-        for k in range(k0, tiles):
-            by = left[k][:, j:j + 1] * inv
-            if k == k0:
-                if r == 7:
-                    continue
-                by = jnp.where(row_ids[:, :1] > r, by, 0.0)
-            left[k] = left[k] - by * up_left
-            right[k] = right[k] - by * up_right
+    for t in range(tiles):
+        base = t * 8
+        lrow = [jnp.broadcast_to(left[t][r:r + 1, :], full) for r in range(8)]
+        rrow = [jnp.broadcast_to(right[t][r:r + 1, :], full) for r in range(8)]
+        entry = {(i, j): jnp.broadcast_to(lrow[i][:, base + j:base + j + 1], full) for i in range(8) for j in range(i, 8)}
+        mult = {}
+        recip = []
+        for j in range(8):
+            root = lax.rsqrt(entry[j, j])
+            inv = root * root
+            recip.append(inv)
+            pairs = {(i, k): entry[j, i] * entry[j, k] for i in range(j + 1, 8) for k in range(i, 8)}
+            for i, k in pairs:
+                entry[i, k] = entry[i, k] - pairs[i, k] * inv
+            for i in range(j + 1, 8):
+                mult[i, j] = entry[j, i] * inv
+                lrow[i] = lrow[i] - mult[i, j] * lrow[j]
+                rrow[i] = rrow[i] - mult[i, j] * rrow[j]
+            factor_ref[pl.ds(base + j, 1), :] = jnp.where(lane_ids[:1] >= base + j, (lrow[j] * root)[:1], 0.0)
+            inv_ref[pl.ds(base + j, 1), :] = (rrow[j] * root)[:1]
+        if t == tiles - 1:
+            break
+        for j in range(7, -1, -1):
+            lrow[j] = lrow[j] * recip[j]
+            rrow[j] = rrow[j] * recip[j]
+            for i in range(7, j, -1):
+                lrow[j] = lrow[j] - mult[i, j] * lrow[i]
+                rrow[j] = rrow[j] - mult[i, j] * rrow[i]
+        for k in range(t + 1, tiles):
+            old = left[k]
+            for j in range(7, -1, -1):
+                by = jnp.broadcast_to(old[:, base + j:base + j + 1], full)
+                left[k] = left[k] - by * lrow[j]
+                right[k] = right[k] - by * rrow[j]
     basis_ref[...] = lax.dot_general(image_ref[...], inv_ref[...], (((1,), (1,)), ((), ())), precision=HIGHEST,
                                      preferred_element_type=jnp.float32)
 
@@ -336,7 +355,7 @@
     dma = pltpu.SemaphoreType.DMA
     gram, image = pl.pallas_call(
         comm_kernel,
-        out_shape=(square, square),
+        out_shape=(pltpu.VMEM((BLK, BLK), f32), pltpu.VMEM((BLK, BLK), f32)),
         in_specs=[pl.BlockSpec(memory_space=pl.ANY)] * 6,
         out_specs=(vmem, vmem),
         scratch_shapes=[
@@ -362,6 +381,8 @@
         name="spread",
     )(sketch, degree.reshape(1, BLK), block_vals.reshape(SLOTS, BLK, BLK), block_rows, block_cols,
       live_count)
+    gram = pltpu.with_memory_space_constraint(gram, pltpu.VMEM)
+    image = pltpu.with_memory_space_constraint(image, pltpu.VMEM)
     nodes = BLK * lax.axis_size("row") * lax.axis_size("col")
     return pl.pallas_call(
         functools.partial(factor_kernel, nodes),

time: 80.2 us -> 72.6 us (0.905)
  Pallas kernels: 78.7 us -> 71.2 us
    pallas_call x1, Pallas kernels: 12.4 us -> 5.52 us  [local(): pl.pallas_call(functools.partial(factor_kernel, nodes), out_shape=(square...]
where the time goes in v3:
time: 72.6 us; the launch traced here: 72.5 us
  Pallas kernels  71.2 us (98%)
  between operations  1.29 us (2%)
    pallas_call x1, Pallas kernels, local(): pl.pallas_call(comm_kernel, out_shape=(pltpu.VMEM((BLK, BLK), f32), pltpu...  65.7 us
    pallas_call x1, Pallas kernels, local(): pl.pallas_call(functools.partial(factor_kernel, nodes), out_shape=(square...  5.52 us

profile of v3, /device:TPU:1, one launch (start us, length us, event | category | flops | bytes accessed | tf_op | source)
XLA Modules:
  0.0 72.5 jit_solution(16716698994403074438)
XLA Ops:
  1.3 65.7 %spread.1 = (f32[128,128]{1,0:T(8,128)S(1)}, f32[128,128]{1,0:T(8,128)S(1)}) custom-call(bf16[128,128]{1,0:T(8,128)(2,1)} %sk_any.1, f32[1,128]{1,0:T(1,128)} %bitcast.3, bf16[16,128,128]{2,1,0:T(8,128)(2,1)} %bitcast.2, s32[1,1,16]{2,1,0:T(1,128)} %rows_any.1, s32[1,1,16]{2,1,0:T(1,128)} %cols_any.1, s32[1,1]{1,0:T(1,128)S(6)} %copy.8.live_any), custom_call_target="tpu_custom_call" | custom-call | tf_op jit(solution)/shard_map/spread/pallas_call | solution.py:356
  66.9 5.5 %orthonormalize.1 = (f32[128,128]{1,0:T(8,128)}, f32[128,128]{1,0:T(8,128)}) custom-call(f32[128,128]{1,0:T(8,128)S(1)} %get-tuple-element.4.gram_ref, f32[128,128]{1,0:T(8,128)S(1)} %get-tuple-element.5.image_ref), custom_call_target="tpu_custom_call" | custom-call | tf_op jit(solution)/shard_map/orthonormalize/pallas_call | solution.py:387

commit v4 on v3

--- a/solution.py
+++ b/solution.py
@@ -14,82 +14,90 @@
 SLOTS = 16
 
 PLAN = (
+    (0, 1, 0, 0, 1, 0, 96),
+    (0, -1, 0, 0, 1, 0, 96),
+    (2, 0, 0, 0, 1, 96, 112),
+    (-2, 0, 0, 0, 1, 112, 128),
+    (0, 3, 0, 0, 1, 0, 96),
+    (0, -3, 0, 0, 1, 0, 96),
     (1, 0, 0, 0, 1, 96, 128),
     (-1, 0, 0, 0, 1, 96, 128),
-    (0, 3, 0, 0, 1, 0, 96),
-    (0, -3, 0, 0, 1, 0, 96),
-    (0, 1, 0, 0, 1, 0, 96),
-    (0, -1, 0, 0, 1, 0, 96),
     (1, 0, 0, 0, 1, 0, 96),
     (-1, 0, 0, 0, 1, 0, 96),
-    (1, 0, -1, 0, 1, 96, 112),
-    (-1, 0, 1, 0, 1, 112, 128),
-    (1, 0, -1, 0, 1, 0, 48),
-    (-1, 0, 1, 0, 1, 48, 96),
-    (0, 3, 0, -3, 1, 0, 96),
-    (0, -3, 0, 3, 1, 0, 96),
-    (0, -1, 0, -3, 1, 0, 96),
-    (0, 1, 0, -3, 1, 0, 96),
-    (0, 3, None, 0, 1, 96, 128),
-    (0, -3, None, 0, 1, 96, 128),
-    (0, 1, 0, 3, 1, 0, 96),
-    (0, -1, 0, 3, 1, 0, 96),
+    (0, 1, 0, -1, 1, 0, 96),
+    (0, -1, 0, 1, 1, 0, 96),
+    (2, 0, 0, 1, 1, 0, 48),
+    (0, 1, None, 0, 1, 96, 128),
+    (0, -1, None, 0, 1, 96, 128),
+    (-2, 0, 0, 1, 1, 48, 96),
+    (2, 0, 0, -1, 1, 0, 48),
+    (-2, 0, 0, -1, 1, 48, 96),
+    (0, 2, 0, -3, 1, 0, 96),
+    (0, -2, 0, 3, 1, 0, 96),
     (1, 0, 0, 1, 1, 0, 96),
     (-1, 0, 0, 1, 1, 0, 96),
     (1, 0, 0, -1, 1, 0, 96),
-    (-1, 0, 0, -1, 1, 0, 96),
-    (0, 1, None, 0, 1, 96, 128),
-    (0, -1, None, 0, 1, 96, 128),
-    (0, 1, 0, -6, 1, 0, 96),
-    (0, -1, 0, 6, 1, 0, 96),
-    (0, -1, 0, -6, 1, 0, 96),
-    (0, 1, 0, 6, 1, 0, 96),
-    (1, 0, 0, -3, 2, 0, 96),
-    (-1, 0, 0, -3, 2, 0, 96),
-    (1, 0, -1, 1, 1, 0, 48),
-    (-1, 0, 1, 1, 1, 48, 96),
-    (1, 0, -1, -1, 1, 0, 48),
-    (-1, 0, 1, -1, 1, 48, 96),
-    (0, 3, None, -3, 1, 96, 128),
-    (0, -3, None, 3, 1, 96, 128),
-    (0, -1, None, -3, 1, 96, 128),
-    (0, 1, None, -3, 1, 96, 128),
-    (0, 1, None, 3, 1, 96, 128),
+    (0, 2, 0, -2, 1, 0, 96),
+    (0, -2, 0, 2, 1, 0, 96),
     (1, 0, 0, 2, 2, 0, 96),
     (-1, 0, 0, 2, 2, 0, 96),
-    (0, -1, None, 3, 1, 96, 128),
-    (1, 0, -1, -3, 2, 0, 48),
-    (-1, 0, 1, -3, 2, 48, 96),
-    (0, 1, 0, -7, 1, 0, 48),
-    (0, -1, 0, 7, 1, 48, 96),
-    (1, 0, 0, 6, 2, 0, 96),
-    (-1, 0, 0, 6, 2, 0, 96),
+    (0, 2, None, -1, 1, 96, 128),
+    (1, 0, 0, -3, 2, 0, 96),
+    (0, -2, None, 1, 1, 96, 128),
+    (-1, 0, 0, -3, 2, 0, 96),
+    (-1, 0, 0, -1, 1, 0, 96),
+    (1, 0, -1, 0, 1, 0, 48),
+    (-1, 0, 1, 0, 1, 48, 96),
+    (0, 3, 0, -5, 1, 0, 48),
+    (0, -3, 0, 5, 1, 48, 96),
+    (0, 2, 0, -5, 1, 0, 96),
+    (0, -2, 0, 5, 1, 0, 96),
+    (0, 2, 0, -4, 1, 0, 96),
+    (0, -2, 0, 4, 1, 0, 96),
     (1, 0, 0, 4, 2, 0, 96),
     (-1, 0, 0, 4, 2, 0, 96),
     (1, 0, 0, -5, 2, 0, 96),
     (-1, 0, 0, -5, 2, 0, 96),
-    (1, 0, 0, -7, 2, 0, 96),
-    (-1, 0, 0, -7, 2, 0, 96),
+    (0, 2, None, -3, 1, 96, 128),
+    (0, -2, None, 3, 1, 96, 128),
+    (0, -1, None, -3, 1, 96, 128),
+    (0, 1, None, 3, 1, 96, 128),
+    (0, 1, None, -3, 1, 96, 128),
+    (0, -1, None, 3, 1, 96, 128),
     (1, 0, -1, 2, 2, 0, 48),
     (-1, 0, 1, 2, 2, 48, 96),
-    (0, 1, None, -6, 1, 96, 128),
-    (0, -1, None, 6, 1, 96, 128),
-    (0, -1, None, -6, 1, 96, 128),
-    (0, 1, None, 6, 1, 96, 128),
-    (1, 0, -1, 6, 2, 0, 48),
-    (-1, 0, 1, 6, 2, 48, 96),
+    (1, 0, -1, -3, 2, 0, 48),
     (1, 0, 0, 8, 1, 0, 96),
     (-1, 0, 0, 8, 1, 0, 96),
+    (1, 0, 0, 7, 1, 0, 96),
+    (-1, 0, 0, 7, 1, 0, 96),
+    (1, 0, 0, -7, 1, 0, 96),
+    (-1, 0, 0, -7, 1, 0, 96),
+    (-1, 0, 1, -3, 2, 48, 96),
+    (1, 0, 0, -6, 1, 0, 96),
+    (1, 0, 0, 6, 1, 0, 96),
+    (-1, 0, 0, 6, 1, 0, 96),
+    (-1, 0, 0, -6, 1, 0, 96),
     (1, 0, -1, 4, 2, 0, 48),
     (-1, 0, 1, 4, 2, 48, 96),
-    (0, 1, None, -7, 1, 96, 112),
-    (0, -1, None, 7, 1, 112, 128),
     (1, 0, -1, -5, 2, 0, 48),
+    (0, 3, None, -5, 1, 96, 112),
+    (0, -3, None, 5, 1, 112, 128),
+    (0, 2, None, -5, 1, 96, 128),
+    (0, -2, None, 5, 1, 96, 128),
+    (0, 1, None, -5, 1, 96, 128),
+    (0, -1, None, 5, 1, 96, 128),
     (-1, 0, 1, -5, 2, 48, 96),
-    (1, 0, -1, -7, 2, 0, 48),
-    (-1, 0, 1, -7, 2, 48, 96),
+    (1, 0, -1, 7, 1, 0, 48),
+    (-1, 0, 1, 7, 1, 48, 96),
+    (1, 0, -1, -7, 1, 0, 48),
+    (-1, 0, 1, -7, 1, 48, 96),
     (1, 0, -1, 8, 1, 0, 48),
+    (1, 0, -1, -6, 1, 0, 48),
+    (-1, 0, 1, 6, 1, 48, 96),
     (-1, 0, 1, 8, 1, 48, 96),
+    (1, 0, -1, 6, 1, 0, 48),
+    (-1, 0, 1, -6, 1, 48, 96),
 )
 N_PLAN = len(PLAN)
 LOW = NZ // 2 - 1
@@ -207,41 +215,43 @@
                                   preferred_element_type=jnp.float32)
 
     chip = x * NY + y
-    me = chip * 2 + core
-    keeper = lax.rem(x + y, 2)
-    owner = core == keeper
-
-    def plane(t):
-        tx, ty = t // NY, lax.rem(t, NY)
-        return tx, ty, lax.rem(tx + ty, 2)
-
-    def scatter(k):
-        t = lax.rem(chip + k, NX * NY)
-        tx, ty, tc = plane(t)
+    owner = core == lax.rem(x + y, 2)
+    spots = sorted(((dx, dy) for dx in range(NX) for dy in range(NY)),
+                   key=lambda d: -min(d[0], NX - d[0]) - min(d[1], NY - d[1]))
+
+    def tile_of(tx, ty):
+        return pl.ds(pl.multiple_of((tx * NY + ty) * 8, 8), 8)
+
+    def scatter(dx, dy):
+        tx, ty = lax.rem(x + dx, NX), lax.rem(y + dy, NY)
+        slot = (dx * NY + dy) * 2 + core
         return pltpu.make_async_remote_copy(
-            src_ref=glocal.at[pl.ds(pl.multiple_of(t * 8, 8), 8), :], dst_ref=rsbuf.at[me],
-            send_sem=rs_s.at[k], recv_sem=rs_r.at[me],
-            device_id=(row_of(ty, z), tx * 2 + tc), device_id_type=MESH)
-
-    for k in list(range(1, NX * NY)):
-        scatter(k).start()
+            src_ref=glocal.at[tile_of(tx, ty), :], dst_ref=rsbuf.at[slot],
+            send_sem=rs_s.at[dx * NY + dy], recv_sem=rs_r.at[slot],
+            device_id=(row_of(ty, z), tx * 2 + lax.rem(tx + ty, 2)), device_id_type=MESH)
+
+    for dx, dy in spots[:-1]:
+        scatter(dx, dy).start()
 
     @pl.when(jnp.logical_not(owner))
     def _():
-        scatter(0).start()
-
-    mine = pl.ds(pl.multiple_of(chip * 8, 8), 8)
+        scatter(0, 0).start()
+
+    mine = tile_of(x, y)
+
+    def collect(slot):
+        pltpu.make_async_remote_copy(
+            src_ref=rsbuf.at[slot], dst_ref=rsbuf.at[slot], send_sem=rs_s.at[0], recv_sem=rs_r.at[slot],
+            device_id=(row, x * 2 + other), device_id_type=MESH).wait_recv()
 
     @pl.when(owner)
     def _():
-        total = glocal[mine, :]
-        for k in range(1, 2 * NX * NY):
-            src = lax.rem(me + k, 2 * NX * NY)
-            pltpu.make_async_remote_copy(
-                src_ref=rsbuf.at[src], dst_ref=rsbuf.at[src], send_sem=rs_s.at[0], recv_sem=rs_r.at[src],
-                device_id=(row, x * 2 + other), device_id_type=MESH).wait_recv()
-        for k in range(1, 2 * NX * NY):
-            total = total + rsbuf[lax.rem(me + k, 2 * NX * NY)]
+        collect(other)
+        total = glocal[mine, :] + rsbuf[other]
+        for dx, dy in spots[-2::-1]:
+            for c in (0, 1):
+                collect((dx * NY + dy) * 2 + c)
+                total = total + rsbuf[(dx * NY + dy) * 2 + c]
         zbuf[z] = total
 
         def along(k):
@@ -262,45 +272,41 @@
             total = total + zbuf[k]
         gram_ref[mine, :] = total
 
-        def back(k):
-            if k == 0:
-                device = (row, x * 2 + other)
-            else:
-                t = lax.rem(chip + k // 2, NX * NY)
-                device = (row_of(lax.rem(t, NY), z), t // NY * 2 + k % 2)
+        def back(dx, dy, c):
+            to = x * 2 + other if (dx, dy) == (0, 0) else lax.rem(x + dx, NX) * 2 + c
             return pltpu.make_async_remote_copy(
-                src_ref=gram_ref.at[mine, :], dst_ref=gram_ref.at[mine, :], send_sem=ag_s.at[k],
-                recv_sem=ag_r.at[chip], device_id=device, device_id_type=MESH)
-
-        spots = [0] + list(range(2, 2 * NX * NY))
-        for k in spots[::-1]:
-            back(k).start()
+                src_ref=gram_ref.at[mine, :], dst_ref=gram_ref.at[mine, :], send_sem=ag_s.at[(dx * NY + dy) * 2 + c],
+                recv_sem=ag_r.at[dx * NY + dy], device_id=(row_of(y + dy, z), to), device_id_type=MESH)
+
+        backs = [(dx, dy, c) for dx, dy in spots for c in (0, 1) if (dx, dy, c) != (0, 0, 0)]
+        for spot in backs:
+            back(*spot).start()
         for k in order:
             along(k).wait_send()
-        for k in spots:
-            back(k).wait_send()
-
-    def arrive(t):
-        lines = pl.ds(pl.multiple_of(t * 8, 8), 8)
+        for spot in backs:
+            back(*spot).wait_send()
+
+    def arrive(dx, dy):
+        lines = tile_of(lax.rem(x - dx + NX, NX), lax.rem(y - dy + NY, NY))
         pltpu.make_async_remote_copy(
             src_ref=gram_ref.at[lines, :], dst_ref=gram_ref.at[lines, :], send_sem=ag_s.at[0],
-            recv_sem=ag_r.at[t], device_id=(row, x * 2 + other), device_id_type=MESH).wait_recv()
-
-    for k in range(1, NX * NY):
-        arrive(lax.rem(chip + k, NX * NY))
+            recv_sem=ag_r.at[dx * NY + dy], device_id=(row, x * 2 + other), device_id_type=MESH).wait_recv()
+
+    for dx, dy in spots[-2::-1]:
+        arrive(dx, dy)
 
     @pl.when(jnp.logical_not(owner))
     def _():
-        arrive(chip)
-        scatter(0).wait_send()
+        arrive(0, 0)
+        scatter(0, 0).wait_send()
 
     for i in range(N_PLAN):
         message(i).wait_send()
     swap.wait_send()
     for send in sends:
         send.wait_send()
-    for k in range(1, NX * NY):
-        scatter(k).wait_send()
+    for dx, dy in spots[:-1]:
+        scatter(dx, dy).wait_send()
 
 
 def factor_kernel(nodes, gram_ref, image_ref, basis_ref, factor_ref, inv_ref):

time: 72.6 us -> 69.8 us (0.961)
  Pallas kernels: 71.2 us -> 68.4 us
    pallas_call x1, Pallas kernels: 65.7 us -> 62.8 us  [local(): pl.pallas_call(comm_kernel, out_shape=(pltpu.VMEM((BLK, BLK), f32), pltpu...]
where the time goes in v4:
time: 69.8 us; the launch traced here: 69.6 us
  Pallas kernels  68.4 us (98%)
  between operations  1.29 us (2%)
    pallas_call x1, Pallas kernels, local(): pl.pallas_call(comm_kernel, out_shape=(pltpu.VMEM((BLK, BLK), f32), pltpu...  62.8 us
    pallas_call x1, Pallas kernels, local(): pl.pallas_call(functools.partial(factor_kernel, nodes), out_shape=(square...  5.53 us

profile of v4, /device:TPU:1, one launch (start us, length us, event | category | flops | bytes accessed | tf_op | source)
XLA Modules:
  0.0 69.6 jit_solution(15338761822453268463)
XLA Ops:
  1.3 62.8 %spread.1 = (f32[128,128]{1,0:T(8,128)S(1)}, f32[128,128]{1,0:T(8,128)S(1)}) custom-call(bf16[128,128]{1,0:T(8,128)(2,1)} %sk_any.1, f32[1,128]{1,0:T(1,128)} %bitcast.3, bf16[16,128,128]{2,1,0:T(8,128)(2,1)} %bitcast.2, s32[1,1,16]{2,1,0:T(1,128)} %rows_any.1, s32[1,1,16]{2,1,0:T(1,128)} %cols_any.1, s32[1,1]{1,0:T(1,128)S(6)} %copy.8.live_any), custom_call_target="tpu_custom_call" | custom-call | tf_op jit(solution)/shard_map/spread/pallas_call | solution.py:362
  64.1 5.5 %orthonormalize.1 = (f32[128,128]{1,0:T(8,128)}, f32[128,128]{1,0:T(8,128)}) custom-call(f32[128,128]{1,0:T(8,128)S(1)} %get-tuple-element.4.gram_ref, f32[128,128]{1,0:T(8,128)S(1)} %get-tuple-element.5.image_ref), custom_call_target="tpu_custom_call" | custom-call | tf_op jit(solution)/shard_map/orthonormalize/pallas_call | solution.py:393

commit v5 on v4

--- a/solution.py
+++ b/solution.py
@@ -14,90 +14,90 @@
 SLOTS = 16
 
 PLAN = (
-    (0, 1, 0, 0, 1, 0, 96),
-    (0, -1, 0, 0, 1, 0, 96),
     (2, 0, 0, 0, 1, 96, 112),
     (-2, 0, 0, 0, 1, 112, 128),
     (0, 3, 0, 0, 1, 0, 96),
     (0, -3, 0, 0, 1, 0, 96),
     (1, 0, 0, 0, 1, 96, 128),
     (-1, 0, 0, 0, 1, 96, 128),
+    (0, 2, 0, 0, 1, 0, 96),
+    (0, -2, 0, 0, 1, 0, 96),
+    (0, 1, 0, 0, 1, 0, 96),
+    (0, -1, 0, 0, 1, 0, 96),
+    (2, 0, 0, 0, 1, 0, 48),
+    (-2, 0, 0, 0, 1, 48, 96),
     (1, 0, 0, 0, 1, 0, 96),
     (-1, 0, 0, 0, 1, 0, 96),
-    (0, 1, 0, -1, 1, 0, 96),
-    (0, -1, 0, 1, 1, 0, 96),
-    (2, 0, 0, 1, 1, 0, 48),
     (0, 1, None, 0, 1, 96, 128),
     (0, -1, None, 0, 1, 96, 128),
-    (-2, 0, 0, 1, 1, 48, 96),
-    (2, 0, 0, -1, 1, 0, 48),
-    (-2, 0, 0, -1, 1, 48, 96),
-    (0, 2, 0, -3, 1, 0, 96),
-    (0, -2, 0, 3, 1, 0, 96),
-    (1, 0, 0, 1, 1, 0, 96),
-    (-1, 0, 0, 1, 1, 0, 96),
-    (1, 0, 0, -1, 1, 0, 96),
-    (0, 2, 0, -2, 1, 0, 96),
-    (0, -2, 0, 2, 1, 0, 96),
-    (1, 0, 0, 2, 2, 0, 96),
-    (-1, 0, 0, 2, 2, 0, 96),
+    (0, 1, 0, -3, 1, 0, 96),
+    (0, -1, 0, 3, 1, 0, 96),
+    (0, 3, 0, -3, 1, 0, 96),
+    (0, -3, 0, 3, 1, 0, 96),
+    (1, 0, 0, 3, 1, 0, 96),
+    (-1, 0, 0, 3, 1, 0, 96),
+    (1, 0, 0, -3, 1, 0, 96),
+    (-1, 0, 0, -3, 1, 0, 96),
+    (1, 0, 0, -2, 2, 0, 96),
+    (1, 0, 0, 1, 2, 0, 96),
+    (-1, 0, 0, 1, 2, 0, 96),
     (0, 2, None, -1, 1, 96, 128),
-    (1, 0, 0, -3, 2, 0, 96),
     (0, -2, None, 1, 1, 96, 128),
-    (-1, 0, 0, -3, 2, 0, 96),
-    (-1, 0, 0, -1, 1, 0, 96),
-    (1, 0, -1, 0, 1, 0, 48),
-    (-1, 0, 1, 0, 1, 48, 96),
-    (0, 3, 0, -5, 1, 0, 48),
-    (0, -3, 0, 5, 1, 48, 96),
-    (0, 2, 0, -5, 1, 0, 96),
-    (0, -2, 0, 5, 1, 0, 96),
-    (0, 2, 0, -4, 1, 0, 96),
-    (0, -2, 0, 4, 1, 0, 96),
-    (1, 0, 0, 4, 2, 0, 96),
-    (-1, 0, 0, 4, 2, 0, 96),
-    (1, 0, 0, -5, 2, 0, 96),
-    (-1, 0, 0, -5, 2, 0, 96),
+    (-1, 0, 0, -2, 2, 0, 96),
+    (0, 1, 0, -4, 1, 0, 96),
+    (0, -1, 0, 4, 1, 0, 96),
+    (0, 3, 0, -4, 1, 0, 96),
+    (0, -3, 0, 4, 1, 0, 96),
+    (2, 0, 0, 4, 1, 0, 48),
+    (-2, 0, 0, 4, 1, 48, 96),
+    (2, 0, 0, -4, 1, 0, 48),
+    (-2, 0, 0, -4, 1, 48, 96),
+    (1, 0, 0, 4, 1, 0, 96),
+    (-1, 0, 0, 4, 1, 0, 96),
+    (1, 0, 0, -4, 1, 0, 96),
+    (-1, 0, 0, -4, 1, 0, 96),
+    (1, 0, -1, -2, 2, 0, 48),
+    (-1, 0, 1, 1, 2, 48, 96),
+    (1, 0, -1, 3, 1, 0, 48),
+    (-1, 0, 1, 3, 1, 48, 96),
     (0, 2, None, -3, 1, 96, 128),
     (0, -2, None, 3, 1, 96, 128),
     (0, -1, None, -3, 1, 96, 128),
+    (0, 3, 0, -5, 1, 0, 48),
+    (0, -3, 0, 5, 1, 48, 96),
+    (1, 0, 0, 5, 2, 0, 96),
+    (-1, 0, 0, 5, 2, 0, 96),
+    (1, 0, 0, -6, 2, 0, 96),
+    (-1, 0, 0, -6, 2, 0, 96),
     (0, 1, None, 3, 1, 96, 128),
     (0, 1, None, -3, 1, 96, 128),
-    (0, -1, None, 3, 1, 96, 128),
-    (1, 0, -1, 2, 2, 0, 48),
-    (-1, 0, 1, 2, 2, 48, 96),
-    (1, 0, -1, -3, 2, 0, 48),
-    (1, 0, 0, 8, 1, 0, 96),
-    (-1, 0, 0, 8, 1, 0, 96),
+    (1, 0, 0, -7, 1, 0, 96),
     (1, 0, 0, 7, 1, 0, 96),
     (-1, 0, 0, 7, 1, 0, 96),
-    (1, 0, 0, -7, 1, 0, 96),
     (-1, 0, 0, -7, 1, 0, 96),
-    (-1, 0, 1, -3, 2, 48, 96),
-    (1, 0, 0, -6, 1, 0, 96),
-    (1, 0, 0, 6, 1, 0, 96),
-    (-1, 0, 0, 6, 1, 0, 96),
-    (-1, 0, 0, -6, 1, 0, 96),
-    (1, 0, -1, 4, 2, 0, 48),
-    (-1, 0, 1, 4, 2, 48, 96),
-    (1, 0, -1, -5, 2, 0, 48),
+    (0, -1, None, 3, 1, 96, 128),
+    (1, 0, -1, 1, 2, 0, 48),
+    (-1, 0, 1, -2, 2, 48, 96),
     (0, 3, None, -5, 1, 96, 112),
     (0, -3, None, 5, 1, 112, 128),
     (0, 2, None, -5, 1, 96, 128),
     (0, -2, None, 5, 1, 96, 128),
     (0, 1, None, -5, 1, 96, 128),
     (0, -1, None, 5, 1, 96, 128),
-    (-1, 0, 1, -5, 2, 48, 96),
+    (1, 0, -1, 5, 2, 0, 48),
+    (-1, 0, 1, 5, 2, 48, 96),
+    (2, 0, 0, 8, 1, 0, 48),
+    (1, 0, -1, -3, 1, 0, 48),
+    (1, 0, -1, -6, 2, 0, 48),
+    (-1, 0, 1, -6, 2, 48, 96),
+    (-1, 0, 1, -3, 1, 48, 96),
+    (-2, 0, 0, 8, 1, 48, 96),
+    (1, 0, 0, 8, 1, 0, 96),
+    (-1, 0, 0, 8, 1, 0, 96),
     (1, 0, -1, 7, 1, 0, 48),
     (-1, 0, 1, 7, 1, 48, 96),
     (1, 0, -1, -7, 1, 0, 48),
     (-1, 0, 1, -7, 1, 48, 96),
-    (1, 0, -1, 8, 1, 0, 48),
-    (1, 0, -1, -6, 1, 0, 48),
-    (-1, 0, 1, 6, 1, 48, 96),
-    (-1, 0, 1, 8, 1, 48, 96),
-    (1, 0, -1, 6, 1, 0, 48),
-    (-1, 0, 1, -6, 1, 48, 96),
 )
 N_PLAN = len(PLAN)
 LOW = NZ // 2 - 1

time: 69.8 us -> 69.7 us (level)
  no operation moved by 1% of the time
where the time goes in v5:
time: 69.7 us; the launch traced here: 69.6 us
  Pallas kernels  68.3 us (98%)
  between operations  1.29 us (2%)
    pallas_call x1, Pallas kernels, local(): pl.pallas_call(comm_kernel, out_shape=(pltpu.VMEM((BLK, BLK), f32), pltpu...  62.8 us
    pallas_call x1, Pallas kernels, local(): pl.pallas_call(functools.partial(factor_kernel, nodes), out_shape=(square...  5.53 us

profile of v5, /device:TPU:1, one launch (start us, length us, event | category | flops | bytes accessed | tf_op | source)
XLA Modules:
  0.0 69.6 jit_solution(3903672868301822286)
XLA Ops:
  1.3 62.8 %spread.1 = (f32[128,128]{1,0:T(8,128)S(1)}, f32[128,128]{1,0:T(8,128)S(1)}) custom-call(bf16[128,128]{1,0:T(8,128)(2,1)} %sk_any.1, f32[1,128]{1,0:T(1,128)} %bitcast.3, bf16[16,128,128]{2,1,0:T(8,128)(2,1)} %bitcast.2, s32[1,1,16]{2,1,0:T(1,128)} %rows_any.1, s32[1,1,16]{2,1,0:T(1,128)} %cols_any.1, s32[1,1]{1,0:T(1,128)S(6)} %copy.8.live_any), custom_call_target="tpu_custom_call" | custom-call | tf_op jit(solution)/shard_map/spread/pallas_call | solution.py:362
  64.1 5.5 %orthonormalize.1 = (f32[128,128]{1,0:T(8,128)}, f32[128,128]{1,0:T(8,128)}) custom-call(f32[128,128]{1,0:T(8,128)S(1)} %get-tuple-element.4.gram_ref, f32[128,128]{1,0:T(8,128)S(1)} %get-tuple-element.5.image_ref), custom_call_target="tpu_custom_call" | custom-call | tf_op jit(solution)/shard_map/orthonormalize/pallas_call | solution.py:393
